TPU v7x, 512 devices: a whole 4x8x8 slice. The times are simulated.
512 devices in a mesh: rep: 4 (over z_hi), dp: 16 (over y, core), tensor: 8 (over x, z_lo).
Axes of the slice: x: 4, y: 8, z: 8 (z_hi: 4, z_lo: 2; z = z_hi * 2 + z_lo), core: 2. Of those that a mesh axis runs over, the one named last changes fastest.
Arguments:
- grad_proj: float32 [64, 3072, 1536], P(('rep', 'dp'), 'tensor'), as said below
- grad_conv: float32 [64, 4, 3328], P(('rep', 'dp'), None, 'tensor'), may hold values from -24 to 24
- param_proj: float32 [3072, 1536], P('tensor', 'dp'), may hold values from -6 to 6
- m_proj: float32 [3072, 1536], P('tensor', 'dp'), may hold values from -2 to 2
- v_proj: float32 [3072, 1536], P('tensor', 'dp'), may hold values from 0.02 to 0.2
- ema_proj: float32 [3072, 1536], P(('tensor', 'dp')), may hold values from -6 to 6
- param_conv: float32 [4, 3328], P(None, 'tensor'), may hold values from -3 to 3
- m_conv: float32 [4, 3328], P(None, 'tensor'), may hold values from -2 to 2
- v_conv: float32 [4, 3328], P(None, 'tensor'), may hold values from 0.02 to 0.2
Outputs:
- new_param_proj: float32 [3072, 1536], P('tensor', 'dp')
- new_m_proj: float32 [3072, 1536], P('tensor', 'dp')
- new_v_proj: float32 [3072, 1536], P('tensor', 'dp')
- new_ema_proj: float32 [3072, 1536], P(('tensor', 'dp'))
- weights_proj: bfloat16 [3072, 1536], P('tensor')
- new_param_conv: float32 [4, 3328], P(None, 'tensor')
- new_m_conv: float32 [4, 3328], P(None, 'tensor')
- new_v_conv: float32 [4, 3328], P(None, 'tensor')
Inputs may be any that keep to these rules, and one draw needn't show every extreme that they name: `grad_proj`: Real-valued gradients with entries of magnitude below 3100.
All inputs are finite; a program needn't handle non-finite values.
Results may differ from a plain program's by a relative error of at most 0.001.
Values may be sent and summed in bfloat16 or wider, within the bound.
A program may use at most 64 MiB of HBM per device.

v0:
```python
import math
import jax
import jax.numpy as jnp
from jax import lax
from jax.sharding import PartitionSpec as P

D = 1536
INNER = 3072
CONV = 3328
KCONV = 4


def adamw_step(param_in, first_in, second_in, grad_in):
    first_out = 0.9 * first_in + 0.1 * grad_in
    second_out = 0.95 * second_in + 0.05 * grad_in * grad_in
    bias_one = 1.0 - 0.9**10
    bias_two = 1.0 - 0.95**10
    update = first_out / bias_one / (jnp.sqrt(second_out / bias_two) + 1e-08)
    param_out = param_in - 0.25 * (update + 0.1 * param_in)
    return (param_out, first_out, second_out)


def clip_from(square_sum):
    clip_limit = 0.5 * math.sqrt(INNER * D + KCONV * CONV)
    return jnp.minimum(1.0, clip_limit / (jnp.sqrt(square_sum) + 1e-06))


def body(grad_proj, grad_conv, param_proj, m_proj, v_proj, ema_proj, param_conv, m_conv, v_conv):
    replica_count = lax.axis_size("rep") * lax.axis_size("dp")
    conv_avg = lax.psum(grad_conv[0], ("rep", "dp")) / replica_count
    conv_square = jnp.sum(conv_avg * conv_avg)
    first_owner = lax.axis_index("dp") == 0
    owner_sum = lax.psum_scatter(grad_proj[0], "dp", scatter_dimension=1, tiled=True)
    proj_avg = lax.psum(owner_sum, "rep") / replica_count
    conv_share = jnp.where(first_owner, conv_square, jnp.float32(0.0))
    square_sum = lax.psum(jnp.sum(proj_avg * proj_avg) + conv_share, ("dp", "tensor"))
    clip_factor = clip_from(square_sum)
    new_param_proj, new_m_proj, new_v_proj = adamw_step(
        param_proj, m_proj, v_proj, clip_factor * proj_avg
    )
    new_param_conv, new_m_conv, new_v_conv = adamw_step(
        param_conv, m_conv, v_conv, clip_factor * conv_avg
    )
    ema_count = ema_proj.shape[0]
    full_block = lax.all_gather(
        new_param_proj.astype(jnp.bfloat16), "dp", axis=1, tiled=True
    ).astype(new_param_proj.dtype)
    weights_proj = full_block.astype(jnp.bfloat16)
    row_block = lax.dynamic_slice_in_dim(full_block, lax.axis_index("dp") * ema_count, ema_count, 0)
    new_ema_proj = 0.9 * ema_proj + 0.1 * row_block
    return (
        new_param_proj,
        new_m_proj,
        new_v_proj,
        new_ema_proj,
        weights_proj,
        new_param_conv,
        new_m_conv,
        new_v_conv,
    )


def solution(mesh):
    in_specs = (
        P(("rep", "dp"), "tensor", None),
        P(("rep", "dp"), None, "tensor"),
        P("tensor", "dp"),
        P("tensor", "dp"),
        P("tensor", "dp"),
        P(("tensor", "dp"), None),
        P(None, "tensor"),
        P(None, "tensor"),
        P(None, "tensor"),
    )
    out_specs = (
        P("tensor", "dp"),
        P("tensor", "dp"),
        P("tensor", "dp"),
        P(("tensor", "dp"), None),
        P("tensor", None),
        P(None, "tensor"),
        P(None, "tensor"),
        P(None, "tensor"),
    )
    return jax.shard_map(body, mesh=mesh, in_specs=in_specs, out_specs=out_specs, check_vma=False)
```

profile of v0, /device:TPU:1, one launch (start us, length us, event | category | flops | bytes accessed | tf_op | source)
XLA Modules:
  0.0 549.1 jit_solution(13845586338401462347)
XLA Ops:
  7.2 0.0 reduce-scatter.2.cloned.1.call-start
  7.2 3.1 copy.19
  10.3 0.0 copy-start.8
  10.3 0.0 copy-start.2
  10.3 0.0 copy-start.3
  10.3 0.0 copy-start.4
  10.3 0.0 reduce-scatter.2.cloned.1.call-update
  10.3 0.0 copy-start.1
  10.3 0.0 all-reduce.2.cloned.1.call-start
  10.4 66.1 %reduce-scatter.2.cloned.1.call-done = f32[384,96]{0,1:T(8,128)} async-done(((f32[384,1536]{0,1:T(8,128)}), f32[384,96]{0,1:T(8,128)}) %reduce-scatter.2.cloned.1.call-update) | async-done | bytes 147472 | tf_op jit(solution)/shard_map/reduce_scatter | solution.py:33
  76.5 0.0 all-reduce.2.cloned.1.call-update
  76.5 0.0 copy-start.5
  76.5 0.0 copy-start.6
  76.5 0.0 copy-start.7
  76.5 0.0 all-gather.2.cloned.1.call-start
  76.6 0.0 copy-done.8
  76.6 142.5 %psum.22 = f32[4,416]{1,0:T(4,128)S(1)} all-reduce(f32[4,416]{1,0:T(4,128)S(1)} %bitcast.3), channel_id=1, replica_groups=mesh['rep'=4,'dp'=16,'tensor'=8] {'rep','dp'}, use_global_device_ids=true, to_apply=%region_3.0 | all-reduce | flops 1664 | bytes 13312 | tf_op jit(solution)/shard_map/psum | solution.py:30
  219.1 0.6 multiply_reduce_fusion.1
  220.3 0.0 all-reduce.2.cloned.1.call-done
  220.4 1.6 multiply_reduce_fusion
  222.6 270.7 %psum.23 = f32[]{:T(128)} all-reduce(f32[]{:T(128)S(6)} %add.50), channel_id=1, replica_groups=mesh['rep'=4,'dp'=16,'tensor'=8] {'dp','tensor'}, use_global_device_ids=true, to_apply=%region_5.6 | all-reduce | flops 1 | bytes 8 | tf_op jit(solution)/shard_map/psum | solution.py:36
  494.0 0.0 copy-done.2
  494.0 0.0 copy-done.3
  494.0 0.0 copy-done.4
  494.0 1.8 fusion.3
  495.7 0.0 all-gather.2.cloned.1.call-update
  495.8 0.0 copy-done.1
  495.8 0.3 copy.20
  496.1 0.0 copy-done.5
  496.1 0.0 copy-done.6
  496.1 0.0 copy-done.7
  496.1 0.6 multiply_subtract_fusion.1
  496.7 42.1 %all-gather.2.cloned.1.call-done = bf16[384,1536]{0,1:T(8,128)(2,1)} async-done(((bf16[384,96]{0,1:T(8,128)(2,1)}), bf16[384,1536]{0,1:T(8,128)(2,1)}) %all-gather.2.cloned.1.call-update) | async-done | bytes 1179664 | tf_op jit(solution)/shard_map/all_gather | solution.py:45
  538.8 0.0 copy-start
  538.8 1.4 multiply_add_fusion
  540.3 0.9 copy.21
  541.2 0.0 copy-done
  541.2 1.4 copy.22
Async XLA Ops:
  7.2 69.3 %reduce-scatter.2.cloned.1.call-start = ((), (), s32[]{:S(2)}) async-start(), calls=%async_computation.1 | async-start | bytes 2506752 | tf_op jit(solution)/shard_map/reduce_scatter | solution.py:33
  10.3 66.3 %copy-start.8 = (f32[1,4,416]{2,1,0:T(4,128)S(1)}, f32[1,4,416]{2,1,0:T(4,128)}, u32[]{:S(2)}) copy-start(f32[1,4,416]{2,1,0:T(4,128)} %param.10) | copy-start | bytes 19972
  10.3 483.7 %copy-start.2 = (f32[384,96]{0,1:T(8,128)S(1)}, f32[384,96]{0,1:T(8,128)}, u32[]{:S(2)}) copy-start(f32[384,96]{0,1:T(8,128)} %param.11) | copy-start | bytes 442372
  10.3 483.7 %copy-start.3 = (f32[384,96]{0,1:T(8,128)S(1)}, f32[384,96]{0,1:T(8,128)}, u32[]{:S(2)}) copy-start(f32[384,96]{0,1:T(8,128)} %param.12) | copy-start | bytes 442372
  10.3 483.7 %copy-start.4 = (f32[384,96]{0,1:T(8,128)S(1)}, f32[384,96]{0,1:T(8,128)}, u32[]{:S(2)}) copy-start(f32[384,96]{0,1:T(8,128)} %param.13) | copy-start | bytes 442372
  10.3 485.4 %copy-start.1 = (f32[24,1536]{1,0:T(8,128)S(1)}, f32[24,1536]{1,0:T(8,128)}, u32[]{:S(2)}) copy-start(f32[24,1536]{1,0:T(8,128)} %param.14) | copy-start | bytes 442372
  10.3 210.0 %all-reduce.2.cloned.1.call-start = ((), (), s32[]{:S(2)}) async-start(), calls=%async_computation.2 | async-start | bytes 294912 | tf_op jit(solution)/shard_map/psum | solution.py:34
  76.5 419.6 %copy-start.5 = (f32[4,416]{1,0:T(4,128)S(1)}, f32[4,416]{1,0:T(4,128)}, u32[]{:S(2)}) copy-start(f32[4,416]{1,0:T(4,128)} %param.15) | copy-start | bytes 19972
  76.5 419.5 %copy-start.6 = (f32[4,416]{1,0:T(4,128)S(1)}, f32[4,416]{1,0:T(4,128)}, u32[]{:S(2)}) copy-start(f32[4,416]{1,0:T(4,128)} %param.16) | copy-start | bytes 19972
  76.5 419.5 %copy-start.7 = (f32[4,416]{1,0:T(4,128)S(1)}, f32[4,416]{1,0:T(4,128)}, u32[]{:S(2)}) copy-start(f32[4,416]{1,0:T(4,128)} %param.17) | copy-start | bytes 19972
  76.5 462.3 %all-gather.2.cloned.1.call-start = ((), (), s32[]{:S(2)}) async-start(), calls=%async_computation.3 | async-start | bytes 1253376 | tf_op jit(solution)/shard_map/all_gather | solution.py:45
  538.8 2.3 copy-start
Sparse Core Ops, SparseCore 0:
  10.8 65.6 reduce-scatter.1
  79.4 55.1 all-reduce.1
  495.9 42.8 all-gather.1
where the time goes:
time: 549 us
  blocking collectives  413 us (75%)
  waiting for transfers between devices  108 us (20%)
  between operations  15.9 us (3%)
  other arithmetic  5.98 us (1%)
  local copies, waits for them, and re-layouts  5.74 us (1%)
    psum x1, blocking collectives, body(): lax.psum(jnp.sum(proj_avg * proj_avg) + conv_share, ('dp', 'tensor'))  271 us
    psum x1, blocking collectives, body(): conv_avg = lax.psum(grad_conv[0], ('rep', 'dp')) / replica_count  142 us
    reduce_scatter x1, waiting for transfers between devices, body(): lax.psum_scatter(grad_proj[0], 'dp', scatter_dimension=1, tiled=True)  66.1 us
    all_gather x1, waiting for transfers between devices, body(): lax.all_gather(new_param_proj.astype(jnp.bfloat16), 'dp', axis=1, tiled=T...  42.1 us
  transfers between devices with their start and end apart: 3, of which 2 were waited for; matrix products, arithmetic and copies ran while one was open for 0% of the time, Pallas kernels for 0%

commit v1 on v0

--- a/solution.py
+++ b/solution.py
@@ -27,7 +27,7 @@
 
 def body(grad_proj, grad_conv, param_proj, m_proj, v_proj, ema_proj, param_conv, m_conv, v_conv):
     replica_count = lax.axis_size("rep") * lax.axis_size("dp")
-    conv_avg = lax.psum(grad_conv[0], ("rep", "dp")) / replica_count
+    conv_avg = jnp.sum(lax.all_gather(grad_conv[0], ("rep", "dp")), axis=0) / replica_count
     conv_square = jnp.sum(conv_avg * conv_avg)
     first_owner = lax.axis_index("dp") == 0
     owner_sum = lax.psum_scatter(grad_proj[0], "dp", scatter_dimension=1, tiled=True)

time: 549 us -> 488 us (0.89)
  blocking collectives: 413 us -> 349 us
    psum x1 -> x0, blocking collectives: 142 us -> none  [body(): conv_avg = lax.psum(grad_conv[0], ('rep', 'dp')) / replica_count]
    all_gather x0 -> x1, blocking collectives: none -> 83.7 us  [body(): lax.all_gather(grad_conv[0], ('rep', 'dp'))]
where the time goes in v1:
time: 488 us; the launch traced here: 487 us
  blocking collectives  349 us (72%)
  waiting for transfers between devices  110 us (23%)
  between operations  15.9 us (3%)
  other arithmetic  6.1 us (1%)
  local copies, waits for them, and re-layouts  5.74 us (1%)
    psum x1, blocking collectives, body(): lax.psum(jnp.sum(proj_avg * proj_avg) + conv_share, ('dp', 'tensor'))  266 us
    all_gather x1, blocking collectives, body(): lax.all_gather(grad_conv[0], ('rep', 'dp'))  83.7 us
    reduce_scatter x1, waiting for transfers between devices, body(): lax.psum_scatter(grad_proj[0], 'dp', scatter_dimension=1, tiled=True)  66.1 us
    all_gather x1, waiting for transfers between devices, body(): lax.all_gather(new_param_proj.astype(jnp.bfloat16), 'dp', axis=1, tiled=T...  44.2 us
  transfers between devices with their start and end apart: 3, of which 2 were waited for; matrix products, arithmetic and copies ran while one was open for 0% of the time, Pallas kernels for 0%

profile of v1, /device:TPU:1, one launch (start us, length us, event | category | flops | bytes accessed | tf_op | source)
XLA Modules:
  0.0 487.5 jit_solution(1015112974493394480)
XLA Ops:
  7.2 0.0 reduce-scatter.2.cloned.1.call-start
  7.2 3.1 copy.19
  10.3 0.0 copy-start.5
  10.3 0.0 reduce-scatter.2.cloned.1.call-update
  10.3 0.0 copy-start.2
  10.3 0.0 copy-start.3
  10.3 0.0 copy-start.4
  10.4 0.0 all-reduce.2.cloned.1.call-start
  10.4 66.1 %reduce-scatter.2.cloned.1.call-done = f32[384,96]{0,1:T(8,128)} async-done(((f32[384,1536]{0,1:T(8,128)}), f32[384,96]{0,1:T(8,128)}) %reduce-scatter.2.cloned.1.call-update) | async-done | bytes 147472 | tf_op jit(solution)/shard_map/reduce_scatter | solution.py:33
  76.5 0.0 all-reduce.2.cloned.1.call-update
  76.5 0.0 copy-start.1
  76.5 0.0 all-gather.2.cloned.1.call-start
  76.6 0.0 copy-done.5
  76.6 83.7 %all_gather.6 = f32[64,4,416]{2,1,0:T(4,128)S(1)} all-gather(f32[1,4,416]{2,1,0:T(4,128)S(1)} %copy-done.5), channel_id=1, replica_groups=mesh['rep'=4,'dp'=16,'tensor'=8] {'rep','dp'}, dimensions={0}, use_global_device_ids=true | all-gather | bytes 432640 | tf_op jit(solution)/shard_map/all_gather | solution.py:30
  160.2 0.1 reduce_sum.28
  160.4 0.0 copy-start.6
  160.4 0.0 copy-start.7
  160.4 0.0 copy-start.8
  160.4 0.6 multiply_reduce_fusion.1
  161.6 0.0 all-reduce.2.cloned.1.call-done
  161.7 1.6 multiply_reduce_fusion
  163.9 265.6 %psum.15 = f32[]{:T(128)} all-reduce(f32[]{:T(128)S(6)} %add.48), channel_id=1, replica_groups=mesh['rep'=4,'dp'=16,'tensor'=8] {'dp','tensor'}, use_global_device_ids=true, to_apply=%region_5.6 | all-reduce | flops 1 | bytes 8 | tf_op jit(solution)/shard_map/psum | solution.py:36
  430.2 0.0 copy-done.2
  430.2 0.0 copy-done.3
  430.2 0.0 copy-done.4
  430.2 1.8 fusion.3
  432.0 0.0 all-gather.2.cloned.1.call-update
  432.0 0.0 copy-done.1
  432.0 0.3 copy.20
  432.3 0.0 copy-done.6
  432.3 0.0 copy-done.7
  432.3 0.0 copy-done.8
  432.3 0.6 multiply_subtract_fusion.1
  432.9 44.2 %all-gather.2.cloned.1.call-done = bf16[384,1536]{0,1:T(8,128)(2,1)} async-done(((bf16[384,96]{0,1:T(8,128)(2,1)}), bf16[384,1536]{0,1:T(8,128)(2,1)}) %all-gather.2.cloned.1.call-update) | async-done | bytes 1179664 | tf_op jit(solution)/shard_map/all_gather | solution.py:45
  477.2 0.0 copy-start
  477.2 1.4 multiply_add_fusion
  478.6 0.9 copy.21
  479.5 0.0 copy-done
  479.5 1.4 copy.22
Async XLA Ops:
  7.2 69.3 %reduce-scatter.2.cloned.1.call-start = ((), (), s32[]{:S(2)}) async-start(), calls=%async_computation.1 | async-start | bytes 2506752 | tf_op jit(solution)/shard_map/reduce_scatter | solution.py:33
  10.3 66.3 %copy-start.5 = (f32[1,4,416]{2,1,0:T(4,128)S(1)}, f32[1,4,416]{2,1,0:T(4,128)}, u32[]{:S(2)}) copy-start(f32[1,4,416]{2,1,0:T(4,128)} %param.10) | copy-start | bytes 19972
  10.3 419.9 %copy-start.2 = (f32[384,96]{0,1:T(8,128)S(1)}, f32[384,96]{0,1:T(8,128)}, u32[]{:S(2)}) copy-start(f32[384,96]{0,1:T(8,128)} %param.11) | copy-start | bytes 442372
  10.3 419.9 %copy-start.3 = (f32[384,96]{0,1:T(8,128)S(1)}, f32[384,96]{0,1:T(8,128)}, u32[]{:S(2)}) copy-start(f32[384,96]{0,1:T(8,128)} %param.12) | copy-start | bytes 442372
  10.3 419.8 %copy-start.4 = (f32[384,96]{0,1:T(8,128)S(1)}, f32[384,96]{0,1:T(8,128)}, u32[]{:S(2)}) copy-start(f32[384,96]{0,1:T(8,128)} %param.13) | copy-start | bytes 442372
  10.4 151.3 %all-reduce.2.cloned.1.call-start = ((), (), s32[]{:S(2)}) async-start(), calls=%async_computation.2 | async-start | bytes 294912 | tf_op jit(solution)/shard_map/psum | solution.py:34
  76.5 355.5 %copy-start.1 = (f32[24,1536]{1,0:T(8,128)S(1)}, f32[24,1536]{1,0:T(8,128)}, u32[]{:S(2)}) copy-start(f32[24,1536]{1,0:T(8,128)} %param.14) | copy-start | bytes 442372
  76.5 400.6 %all-gather.2.cloned.1.call-start = ((), (), s32[]{:S(2)}) async-start(), calls=%async_computation.3 | async-start | bytes 1253376 | tf_op jit(solution)/shard_map/all_gather | solution.py:45
  160.4 271.9 %copy-start.6 = (f32[4,416]{1,0:T(4,128)S(1)}, f32[4,416]{1,0:T(4,128)}, u32[]{:S(2)}) copy-start(f32[4,416]{1,0:T(4,128)} %param.15) | copy-start | bytes 19972
  160.4 271.9 %copy-start.7 = (f32[4,416]{1,0:T(4,128)S(1)}, f32[4,416]{1,0:T(4,128)}, u32[]{:S(2)}) copy-start(f32[4,416]{1,0:T(4,128)} %param.16) | copy-start | bytes 19972
  160.4 271.9 %copy-start.8 = (f32[4,416]{1,0:T(4,128)S(1)}, f32[4,416]{1,0:T(4,128)}, u32[]{:S(2)}) copy-start(f32[4,416]{1,0:T(4,128)} %param.17) | copy-start | bytes 19972
  477.2 2.3 copy-start
Sparse Core Ops, SparseCore 0:
  10.8 65.6 reduce-scatter.1
  79.4 55.2 all-reduce.1
  432.1 44.9 all-gather.1
